TPU v7x, 32 devices: a whole 2x2x4 slice. The times are simulated.
32 devices in a mesh: rep: 8 (over z, x), shard: 4 (over y, core).
Axes of the slice: x: 2, y: 2, z: 4, core: 2. Of those that a mesh axis runs over, the one named last changes fastest.
Arguments:
- inputs: bfloat16 [3072, 1024], P('rep', 'shard'), may hold values from -6 to 6
- cotangent: bfloat16 [3072, 512], P('rep'), may hold values from -0.15625 to 0.15625
- momentum: float32 [512, 1024], P('rep', 'shard'), may hold values from -54 to 54
- right_prev: float32 [1024, 64], P('shard'), may hold values from -0.1875 to 0.1875
Outputs:
- new_momentum: float32 [512, 1024], P('rep', 'shard')
- right_factor: float32 [1024, 64], P('shard')
- update: bfloat16 [512, 1024], P('rep', 'shard')
All inputs are finite; a program needn't handle non-finite values.
Results may differ from a plain program's by a relative error of at most 0.001.
Values sent between devices are 32-bit elements; how exact they have to be, the bound alone decides.
A program may use at most 64 MiB of HBM per device.

v0:
```python
import jax
import jax.numpy as jnp
from jax import lax
from jax.sharding import PartitionSpec as P


def body(inputs, cotangent, momentum, right_prev):
    high = lax.Precision.HIGHEST
    col_count = momentum.shape[1]
    out_total = cotangent.shape[1]
    in_total = col_count * lax.axis_size("shard")
    rank_size = right_prev.shape[1]
    gradient = lax.psum_scatter(
        lax.dot_general(
            cotangent, inputs, (((0,), (0,)), ((), ())), preferred_element_type=jnp.float32
        ),
        "rep",
        scatter_dimension=0,
        tiled=True,
    )
    blended = momentum + gradient
    left_raw = lax.psum(jnp.dot(blended, right_prev, precision=high), "shard")
    gram_sum = lax.psum(jnp.dot(left_raw.T, left_raw, precision=high), "rep")
    lower_factor = jnp.linalg.cholesky(gram_sum)
    ortho = lax.linalg.triangular_solve(lower_factor, left_raw.T, left_side=True, lower=True).T
    local_right = jnp.dot(blended.T, ortho, precision=high)
    right_raw = lax.psum(local_right, "rep")
    column_sq = lax.psum(jnp.sum(right_raw * right_raw, axis=0), "shard")
    new_momentum = blended - 0.05 * jnp.dot(ortho, right_raw.T, precision=high)
    right_factor = right_raw / jnp.sqrt(column_sq + 1e-06)
    scale_factor = (out_total * in_total / rank_size) ** 0.5
    update = (scale_factor * jnp.dot(ortho, right_factor.T, precision=high)).astype(jnp.bfloat16)
    return (new_momentum, right_factor, update)


def solution(mesh):
    return jax.shard_map(
        body,
        mesh=mesh,
        in_specs=(P("rep", "shard"), P("rep", None), P("rep", "shard"), P("shard", None)),
        out_specs=(P("rep", "shard"), P("shard", None), P("rep", "shard")),
        check_vma=False,
    )
```

profile of v0, /device:TPU:0, one launch (start us, length us, event | category | flops | bytes accessed | tf_op | source)
XLA Modules:
  0.0 219.4 jit_solution(16988871786383340574)
XLA Ops:
  7.2 0.0 copy-start
  7.2 0.0 reduce-scatter.2.cloned.1.call-start
  7.2 0.9 copy-done
  8.2 2.1 fusion.6
  10.2 0.0 copy-start.3
  10.2 0.0 reduce-scatter.2.cloned.1.call-update
  10.2 0.0 copy-start.4
  10.3 0.0 all-reduce.2.cloned.1.call-start
  10.3 66.9 %reduce-scatter.2.cloned.1.call-done = f32[64,256]{1,0:T(8,128)} async-done(((f32[512,256]{1,0:T(8,128)}), f32[64,256]{1,0:T(8,128)}) %reduce-scatter.2.cloned.1.call-update) | async-done | bytes 65552 | tf_op jit(solution)/shard_map/reduce_scatter | solution.py:13
  77.2 0.0 copy-done.3
  77.2 0.8 add.30
  78.0 0.0 copy-done.4
  78.0 0.2 fusion.7
  78.3 10.3 %psum.28 = f32[64,64]{1,0:T(8,128)S(1)} all-reduce(f32[64,64]{1,0:T(8,128)S(1)} %fusion.7), channel_id=1, replica_groups=mesh['rep'=8,'shard'=4] {'shard'}, use_global_device_ids=true, to_apply=%region_1.0 | all-reduce | flops 4096 | bytes 32768 | tf_op jit(solution)/shard_map/psum | solution.py:22
  88.5 0.2 fusion.8
  88.8 35.1 %psum.29 = f32[64,64]{0,1:T(8,128)S(1)} all-reduce(f32[64,64]{0,1:T(8,128)S(1)} %fusion.8), channel_id=1, replica_groups=mesh['rep'=8,'shard'=4] {'rep'}, use_global_device_ids=true, to_apply=%region_2.0 | all-reduce | flops 4096 | bytes 32768 | tf_op jit(solution)/shard_map/psum | solution.py:23
  123.9 0.1 copy.8
  124.0 5.9 %cholesky.16 = f32[64,64]{1,0:T(8,128)S(1)} custom-call(f32[64,64]{1,0:T(8,128)S(1)} %fusion.5), custom_call_target="Cholesky" | custom-call | tf_op jit(solution)/shard_map/jit(cholesky)/cholesky | solution.py:24
  129.9 0.6 compare_reduce_fusion
  130.5 0.7 fusion.2
  131.2 4.9 %custom-call.6 = f32[1,64,64]{1,2,0:T(8,128)S(1)} custom-call(f32[1,64,64]{2,1,0:T(8,128)S(1)} %fusion.2), custom_call_target="InvertDiagBlocksLowerTriangular" | custom-call | tf_op jit(solution)/shard_map/triangular_solve | solution.py:25
  136.1 0.2 fusion.3
  136.3 0.8 fusion.9
  137.2 0.0 all-reduce.2.cloned.1.call-update
  137.2 66.8 %all-reduce.2.cloned.1.call-done = f32[256,64]{0,1:T(8,128)} async-done(((f32[256,64]{0,1:T(8,128)}), f32[256,64]{0,1:T(8,128)}) %all-reduce.2.cloned.1.call-update) | async-done | bytes 65552 | tf_op jit(solution)/shard_map/psum | solution.py:27
  204.0 0.0 copy-start.1
  204.0 1.0 multiply_reduce_fusion
  205.0 5.7 %psum.31 = f32[64]{0:T(128)S(1)} all-reduce(f32[64]{0:T(128)S(1)} %multiply_reduce_fusion), channel_id=1, replica_groups=mesh['rep'=8,'shard'=4] {'shard'}, use_global_device_ids=true, to_apply=%region_7.8 | all-reduce | flops 64 | bytes 512 | tf_op jit(solution)/shard_map/psum | solution.py:28
  210.7 0.0 copy-done.1
  210.7 0.1 broadcast_divide_fusion
  210.8 0.0 copy-start.2
  210.8 0.9 fusion.1
  211.7 0.0 copy-done.2
  211.7 0.9 fusion
  (3 shorter events, 0.0 us)
Async XLA Ops:
  7.2 1.0 copy-start
  7.2 70.0 %reduce-scatter.2.cloned.1.call-start = ((), (), s32[]{:S(2)}) async-start(), calls=%async_computation.1 | async-start | bytes 589824 | tf_op jit(solution)/shard_map/reduce_scatter | solution.py:13
  10.2 67.0 %copy-start.3 = (f32[64,256]{1,0:T(8,128)S(1)}, f32[64,256]{1,0:T(8,128)}, u32[]{:S(2)}) copy-start(f32[64,256]{1,0:T(8,128)} %param.6) | copy-start | bytes 196612
  10.2 67.8 %copy-start.4 = (f32[256,64]{0,1:T(8,128)S(1)}, f32[256,64]{0,1:T(8,128)}, u32[]{:S(2)}) copy-start(f32[256,64]{0,1:T(8,128)} %param.7) | copy-start | bytes 196612
  10.3 193.7 %all-reduce.2.cloned.1.call-start = ((), (), s32[]{:S(2)}) async-start(), calls=%async_computation.2 | async-start | bytes 131072 | tf_op jit(solution)/shard_map/psum | solution.py:27
  204.0 6.7 %copy-start.1 = (f32[256,64]{0,1:T(8,128)S(1)}, f32[256,64]{0,1:T(8,128)}, u32[]{:S(2)}) copy-start(f32[256,64]{0,1:T(8,128)} %all-reduce.2.cloned.1.call-done) | copy-start | bytes 196612
  210.8 0.9 copy-start.2
Sparse Core Ops, SparseCore 0:
  11.3 65.8 reduce-scatter.1
  137.3 66.6 all-reduce.1
where the time goes:
time: 220 us; the launch traced here: 219 us
  waiting for transfers between devices  134 us (61%)
  blocking collectives  51.1 us (23%)
  other arithmetic  14.1 us (6%)
  between operations  14.1 us (6%)
  matrix products  5.31 us (2%)
    reduce_scatter x1, waiting for transfers between devices, body(): lax.psum_scatter(lax.dot_general(cotangent, inputs, (((0,), (0,)), ((), (...  66.9 us
    psum x1, waiting for transfers between devices, body(): right_raw = lax.psum(local_right, 'rep')  66.8 us
    psum x1, blocking collectives, body(): gram_sum = lax.psum(jnp.dot(left_raw.T, left_raw, precision=high), 'rep')  35.1 us
    psum x1, blocking collectives, body(): left_raw = lax.psum(jnp.dot(blended, right_prev, precision=high), 'shard')  10.3 us
    another operation x3, other arithmetic, body(): lower_factor = jnp.linalg.cholesky(gram_sum)  6.53 us
    psum x1, blocking collectives, body(): column_sq = lax.psum(jnp.sum(right_raw * right_raw, axis=0), 'shard')  5.67 us
    another operation x2, other arithmetic, body(): lax.linalg.triangular_solve(lower_factor, left_raw.T, left_side=True, low...  5.57 us
  transfers between devices with their start and end apart: 2, of which 2 were waited for; matrix products, arithmetic and copies ran while one was open for 0% of the time, Pallas kernels for 0%

commit v1 on v0

v1 whole, which is shorter than its diff:
```python
import functools

import jax
import jax.numpy as jnp
from jax import lax
from jax.experimental import pallas as pl
from jax.experimental.pallas import tpu as pltpu
from jax.sharding import PartitionSpec as P

MESH = pl.DeviceIdType.MESH
F32, BF16 = jnp.float32, jnp.bfloat16
SUB, LANE = 8, 128
NT = (((1,), (1,)), ((), ()))
NN = (((1,), (0,)), ((), ()))
TN = (((0,), (0,)), ((), ()))


def split(x):
    hi = x.astype(BF16)
    lo = (x - hi.astype(F32)).astype(BF16)
    return jnp.concatenate([hi, lo], axis=0)


def dot_split(x, y, dims):
    rows = x.shape[0]
    both = lax.dot_general(split(x), y, dims, preferred_element_type=F32)
    return both[:rows] + both[rows:]


def dot_high(x, y, dims):
    return lax.dot_general(x, y, dims, precision=lax.Precision.HIGHEST, preferred_element_type=F32)


def inverse_factor(gram):
    size = gram.shape[0]
    row_at = lax.broadcasted_iota(jnp.int32, (size, size), 0)
    col_at = lax.broadcasted_iota(jnp.int32, (size, size), 1)
    eye = jnp.where(row_at == col_at, 1.0, 0.0).astype(F32)
    aug = jnp.concatenate([gram, eye], axis=1)
    width = 2 * size
    count = size // SUB
    blocks = [aug[SUB * i : SUB * (i + 1)] for i in range(count)]
    inner = lax.broadcasted_iota(jnp.int32, (SUB, width), 0)
    outs = []
    for b in range(count):
        cols = [
            [jnp.broadcast_to(blocks[i][:, SUB * b + k : SUB * b + k + 1], (SUB, width)) for i in range(b, count)]
            for k in range(SUB)
        ]
        top = blocks[b]
        scale = jnp.zeros((SUB, width), F32)
        rest = blocks[b + 1 :]
        for k in range(SUB):
            pivot = jnp.broadcast_to(cols[k][0][k : k + 1], (SUB, width))
            inv = 1.0 / pivot
            scale = jnp.where(inner == k, lax.rsqrt(pivot), scale)
            factors = [jnp.where(inner > k, cols[k][0], 0.0)] + cols[k][1:]
            for l in range(k + 1, SUB):
                mult = jnp.broadcast_to(cols[l][0][k : k + 1], (SUB, width)) * inv
                cols[l] = [c - f * mult for c, f in zip(cols[l], factors)]
            row = jnp.broadcast_to(top[k : k + 1], (SUB, width)) * inv
            top = top - factors[0] * row
            rest = [r - f * row for r, f in zip(rest, factors[1:])]
        outs.append((top * scale)[:, size:])
        blocks = blocks[: b + 1] + rest
    return jnp.concatenate(outs, axis=0)


def kernel(
    n_rep, n_shard, scale_factor,
    x_ref, c_ref, m_ref, q_ref,
    mom_out, right_out, up_out,
    left_part, left_in, left, ortho, right_part, right_in, right, sq_in, grad_part, grad_in, pad, turn,
    send, recv,
):
    rep, shard = lax.axis_index("rep"), lax.axis_index("shard")
    n_dev = n_rep * n_shard
    me = rep * n_shard + shard
    rank = q_ref.shape[1]
    out_total = c_ref.shape[1]
    rows, feats = m_ref.shape
    row_blocks = rank // SUB
    left_owners = row_blocks * (out_total // LANE)
    right_owners = row_blocks
    chunk = min(512, out_total)
    n_chunk = out_total // chunk
    per_tile = LANE // rows

    def device(index):
        return (index // n_shard, lax.rem(index, n_shard))

    def guarded(owners, total, index, fn):
        if owners == total:
            fn()
        else:
            pl.when(index < owners)(fn)

    def over(count, fn):
        if count == 1:
            fn(0)
        else:
            lax.fori_loop(0, count, lambda i, u: (fn(i), u)[1], 0)

    def lanes(i):
        if isinstance(i, int):
            return pl.ds(i * chunk, chunk)
        return pl.ds(pl.multiple_of(i * chunk, chunk), chunk)

    def copy(src, dst, k, target):
        return pltpu.make_async_remote_copy(
            src_ref=src, dst_ref=dst, send_sem=send.at[k], recv_sem=recv.at[k],
            device_id=target, device_id_type=MESH,
        )

    def drain(sem, ref):
        pltpu.make_async_copy(ref, ref, sem).wait()

    def tile(ref, t):
        r = pl.multiple_of(lax.rem(t, row_blocks) * SUB, SUB)
        c = pl.multiple_of((t // row_blocks) * LANE, LANE)
        return ref.at[pl.ds(r, SUB), pl.ds(c, LANE)]

    def band(b):
        return pl.ds(pl.multiple_of(b * SUB, SUB), SUB)

    barrier = pltpu.get_barrier_semaphore()

    def greet(p, u):
        pl.semaphore_signal(barrier, inc=1, device_id=device(lax.rem(me + p, n_dev)), device_id_type=MESH)
        return u

    lax.fori_loop(1, n_dev, greet, 0)

    x = x_ref[...]
    q_t = q_ref[...].T
    w_t = dot_split(q_t, x, NT)
    w_two = split(w_t)

    def left_chunk(i):
        both = lax.dot_general(w_two, c_ref[:, lanes(i)], NN, preferred_element_type=F32)
        left_part[:, lanes(i)] = both[:rank] + both[rank:]

    over(n_chunk, left_chunk)
    pad[...] = jnp.zeros_like(pad)
    half = lax.rem(rep, per_tile)
    my_rows = pl.ds(pl.multiple_of(half * rows, rows), rows)
    my_lanes = pl.ds(pl.multiple_of((rep // per_tile) * LANE, LANE), LANE)
    pad[my_rows, :] = m_ref[...]
    left_part[:, my_lanes] += dot_high(q_t, pad[...], NT)

    pl.semaphore_wait(barrier, n_dev - 1)

    def send_left(p, u):
        t = lax.rem(me + p, n_dev)
        guarded(left_owners, n_dev, t, lambda: copy(tile(left_part, t), left_in.at[me], 0, device(t)).start())
        return u

    lax.fori_loop(1, n_dev, send_left, 0)

    def grad_chunk(i):
        g = lax.dot_general(c_ref[:, lanes(i)], x, TN, preferred_element_type=F32)
        grad_part[lanes(i), :] = g

    over(n_chunk, grad_chunk)

    def own_left():
        left_in[me] = tile(left_part, me)[...]
        drain(recv.at[0], left_in.at[pl.ds(0, n_dev - 1)])
        tile(left, me)[...] = jnp.sum(left_in[...], axis=0)

        def give(p, u):
            copy(tile(left, me), tile(left, me), 1, device(lax.rem(me + p, n_dev))).start()
            return u

        lax.fori_loop(1, n_dev, give, 0)

    guarded(left_owners, n_dev, me, own_left)

    def grad_rows(r):
        return pl.ds(pl.multiple_of(r * rows, rows), rows)

    def send_grad(p, u):
        t = lax.rem(rep + p, n_rep)
        copy(grad_part.at[grad_rows(t), :], grad_in.at[rep], 2, (t, shard)).start()
        return u

    if left_owners == n_dev:
        drain(recv.at[1], left_in.at[pl.ds(0, n_dev - 1)])
        lax.fori_loop(1, n_rep, send_grad, 0)
    else:
        lax.fori_loop(1, n_rep, send_grad, 0)

        @pl.when(me < left_owners)
        def _():
            drain(recv.at[1], left_in.at[pl.ds(0, left_owners - 1)])

        @pl.when(me >= left_owners)
        def _():
            drain(recv.at[1], left_in.at[pl.ds(0, left_owners)])

    grad_in[rep] = grad_part[grad_rows(rep), :]

    if n_chunk == 1:
        whole = left[...]
        gram = dot_high(whole, whole, NT)
    else:
        gram = lax.fori_loop(
            0, n_chunk,
            lambda i, g: g + dot_high(left[:, lanes(i)], left[:, lanes(i)], NT),
            jnp.zeros((rank, rank), F32),
        )
    inv = inverse_factor(gram)

    def ortho_chunk(i):
        ortho[:, lanes(i)] = dot_high(inv, left[:, lanes(i)], NN)

    over(n_chunk, ortho_chunk)
    if n_chunk == 1:
        v_t = dot_split(ortho[...], c_ref[...], NT)
    else:
        v_t = lax.fori_loop(
            0, n_chunk,
            lambda i, v: v + dot_split(ortho[:, lanes(i)], c_ref[:, lanes(i)], NT),
            jnp.zeros((rank, c_ref.shape[0]), F32),
        )
    mine_t = ortho[:, my_lanes]
    right_part[...] = dot_split(v_t, x, NN) + dot_high(
        mine_t, pad[...], NN
    )

    def send_right(p, u):
        t = lax.rem(rep + p, n_rep)
        guarded(
            right_owners, n_rep, t,
            lambda: copy(right_part.at[band(t), :], right_in.at[rep], 3, (t, shard)).start(),
        )
        return u

    lax.fori_loop(1, n_rep, send_right, 0)
    pad_turn = mine_t.T

    def own_right():
        right_in[rep] = right_part[band(rep), :]
        drain(recv.at[3], right_in.at[pl.ds(0, n_rep - 1)])
        total = jnp.sum(right_in[...], axis=0)
        right[band(rep), :] = total
        sq_in[shard, band(rep), :] = jnp.broadcast_to(jnp.sum(total * total, axis=1, keepdims=True), (SUB, LANE))

        def give_right(p, u):
            copy(right.at[band(rep), :], right.at[band(rep), :], 4, (lax.rem(rep + p, n_rep), shard)).start()
            return u

        lax.fori_loop(1, n_rep, give_right, 0)

        def give_sq(p, u):
            place = sq_in.at[shard, band(rep), :]
            copy(place, place, 5, device(lax.rem(me + p, n_dev))).start()
            return u

        lax.fori_loop(1, n_dev, give_sq, 0)

    guarded(right_owners, n_rep, rep, own_right)

    drain(recv.at[2], grad_in.at[pl.ds(0, n_rep - 1)])
    blended = m_ref[...] + lax.fori_loop(1, n_rep, lambda r, g: g + grad_in[r], grad_in[0])
    turn[...] = pad_turn
    mine = turn[my_rows, :]

    def finish_recv(n_right, n_sq):
        drain(recv.at[4], right_in.at[pl.ds(0, n_right)])
        flat = left_in.at[pl.ds(0, n_sq)]
        drain(recv.at[5], flat)

    sq_all = right_owners * n_shard
    if right_owners == n_rep:
        finish_recv(right_owners - 1, sq_all - 1)
    else:
        @pl.when(rep < right_owners)
        def _():
            finish_recv(right_owners - 1, sq_all - 1)

        @pl.when(rep >= right_owners)
        def _():
            finish_recv(right_owners, sq_all)

    right_t = right[...]
    mom_out[...] = blended - 0.05 * dot_high(mine, right_t, NN)
    norm = jnp.sqrt(jnp.sum(sq_in[...], axis=0) + 1e-06)
    factor_t = jnp.concatenate(
        [right_t[:, LANE * i : LANE * (i + 1)] / norm for i in range(feats // LANE)], axis=1
    )
    up_out[...] = (scale_factor * dot_high(mine, factor_t, NN)).astype(up_out.dtype)
    right_out[...] = factor_t.T

    def left_sent(n):
        drain(send.at[0], left_in.at[pl.ds(0, n)])

    if left_owners == n_dev:
        left_sent(n_dev - 1)
        drain(send.at[1], left_in.at[pl.ds(0, n_dev - 1)])
    else:
        @pl.when(me < left_owners)
        def _():
            left_sent(left_owners - 1)
            drain(send.at[1], left_in.at[pl.ds(0, n_dev - 1)])

        @pl.when(me >= left_owners)
        def _():
            left_sent(left_owners)

    drain(send.at[2], grad_in.at[pl.ds(0, n_rep - 1)])

    def right_sent():
        drain(send.at[4], right_in.at[pl.ds(0, n_rep - 1)])
        drain(send.at[5], left_in.at[pl.ds(0, n_dev - 1)])

    if right_owners == n_rep:
        drain(send.at[3], right_in.at[pl.ds(0, n_rep - 1)])
        right_sent()
    else:
        @pl.when(rep < right_owners)
        def _():
            drain(send.at[3], right_in.at[pl.ds(0, right_owners - 1)])
            right_sent()

        @pl.when(rep >= right_owners)
        def _():
            drain(send.at[3], right_in.at[pl.ds(0, right_owners)])


def body(n_rep, n_shard, inputs, cotangent, momentum, right_prev):
    out_total = cotangent.shape[1]
    rows, feats = momentum.shape
    rank = right_prev.shape[1]
    n_dev = n_rep * n_shard
    scale_factor = (out_total * feats * n_shard / rank) ** 0.5
    vmem = pl.BlockSpec(memory_space=pltpu.VMEM)
    return pl.pallas_call(
        functools.partial(kernel, n_rep, n_shard, scale_factor),
        out_shape=(
            jax.ShapeDtypeStruct((rows, feats), F32),
            jax.ShapeDtypeStruct((feats, rank), F32),
            jax.ShapeDtypeStruct((rows, feats), BF16),
        ),
        in_specs=[vmem] * 4,
        out_specs=(vmem,) * 3,
        scratch_shapes=[
            pltpu.VMEM((rank, out_total), F32),
            pltpu.VMEM((n_dev, SUB, LANE), F32),
            pltpu.VMEM((rank, out_total), F32),
            pltpu.VMEM((rank, out_total), F32),
            pltpu.VMEM((rank, feats), F32),
            pltpu.VMEM((n_rep, SUB, feats), F32),
            pltpu.VMEM((rank, feats), F32),
            pltpu.VMEM((n_shard, rank, LANE), F32),
            pltpu.VMEM((out_total, feats), F32),
            pltpu.VMEM((n_rep, rows, feats), F32),
            pltpu.VMEM((LANE, feats), F32),
            pltpu.VMEM((LANE, rank), F32),
            pltpu.SemaphoreType.DMA((6,)),
            pltpu.SemaphoreType.DMA((6,)),
        ],
        compiler_params=pltpu.CompilerParams(
            collective_id=0, has_side_effects=True, vmem_limit_bytes=48 * 1024 * 1024
        ),
    )(inputs, cotangent, momentum, right_prev)


def solution(mesh):
    return jax.shard_map(
        functools.partial(body, mesh.shape["rep"], mesh.shape["shard"]),
        mesh=mesh,
        in_specs=(P("rep", "shard"), P("rep", None), P("rep", "shard"), P("shard", None)),
        out_specs=(P("rep", "shard"), P("shard", None), P("rep", "shard")),
        check_vma=False,
    )
```

time: 220 us -> 44.2 us (0.20)
  waiting for transfers between devices: 134 us -> 0 us
  blocking collectives: 51.1 us -> 0 us
  Pallas kernels: 0 us -> 38.6 us
  other arithmetic: 14.1 us -> 0 us
  between operations: 14.1 us -> 0.67 us
  matrix products: 5.31 us -> 0 us
  local copies, waits for them, and re-layouts: 1.05 us -> 4.76 us
    reduce_scatter x1 -> x0, waiting for transfers between devices: 66.9 us -> none  [body(): lax.psum_scatter(lax.dot_general(cotangent, inputs, (((0,), (0,)), ((), (...]
    psum x1 -> x0, waiting for transfers between devices: 66.8 us -> none  [body(): right_raw = lax.psum(local_right, 'rep')]
    psum x3 -> x0, blocking collectives: 51.1 us -> none  [the longest x1 35.1 us: body(): gram_sum = lax.psum(jnp.dot(left_raw.T, left_raw, precision=high), 'rep')]
    pallas_call x0 -> x1, Pallas kernels: none -> 38.6 us  [body(): pl.pallas_call(functools.partial(kernel, n_rep, n_shard, scale_factor), o...]
    another operation x5 -> x0, other arithmetic: 12.1 us -> none  [the longest x3 6.53 us: body(): lower_factor = jnp.linalg.cholesky(gram_sum)]
    dot_general x6 -> x0, matrix products: 5.08 us -> none  [the longest x1 2.05 us: body(): lax.dot_general(cotangent, inputs, (((0,), (0,)), ((), ())), preferred_el...]
    unnamed x10 -> x9, local copies, waits for them, and re-layouts: 0.97 us -> 4.05 us
  transfers between devices with their start and end apart: 2 -> 0, of which waited for: 2 -> 0; matrix products, arithmetic and copies ran while one was open for 0% -> 0% of each run, Pallas kernels for 0% -> 0%
where the time goes in v1:
time: 44.2 us; the launch traced here: 44 us
  Pallas kernels  38.6 us (87%)
  local copies, waits for them, and re-layouts  4.76 us (11%)
  between operations  0.67 us (2%)
    pallas_call x1, Pallas kernels, body(): pl.pallas_call(functools.partial(kernel, n_rep, n_shard, scale_factor), o...  38.6 us
    unnamed x9, local copies, waits for them, and re-layouts  4.05 us

profile of v1, /device:TPU:0, one launch (start us, length us, event | category | flops | bytes accessed | tf_op | source)
XLA Modules:
  0.0 44.0 jit_solution(2279634133101215322)
XLA Ops:
  0.6 0.0 copy-start.1
  0.6 1.0 %copy.7.q_ref = f32[256,64]{1,0:T(8,128)S(1)} copy(f32[256,64]{0,1:T(8,128)} %param.7) | data formatting | bytes 131072 | tf_op args[3]
  1.6 0.0 copy-done.1
  1.6 0.0 copy-start
  1.6 1.0 %copy-done = bf16[384,512]{1,0:T(8,128)(2,1)S(1)} copy-done((bf16[384,512]{1,0:T(8,128)(2,1)S(1)}, bf16[384,512]{1,0:T(8,128)(2,1)}, u32[]{:S(2)}) %copy-start) | copy-done | bytes 393240
  2.6 0.0 copy-start.2
  2.6 0.8 %copy-done.2 = f32[64,256]{1,0:T(8,128)S(1)} copy-done((f32[64,256]{1,0:T(8,128)S(1)}, f32[64,256]{1,0:T(8,128)}, u32[]{:S(2)}) %copy-start.2) | copy-done | bytes 65560
  3.5 38.6 %shard_map.67 = (f32[64,256]{1,0:T(8,128)S(1)}, f32[256,64]{1,0:T(8,128)S(1)}, bf16[64,256]{1,0:T(8,128)(2,1)S(1)}) custom-call(bf16[384,256]{1,0:T(8,128)(2,1)S(1)} %copy-done.1, bf16[384,512]{1,0:T(8,128)(2,1)S(1)} %copy-done, f32[64,256]{1,0:T(8,128)S(1)} %copy-done.2, f32[256,64]{1,0:T(8,128)S(1)} %copy.7.q_ref), custom_call_target="tpu_custom_call" | custom-call | tf_op jit(solution)/shard_map/pallas_call | solution.py:338
  42.1 0.7 %copy.8 = f32[256,64]{0,1:T(8,128)} copy(f32[256,64]{1,0:T(8,128)S(1)} %get-tuple-element.4) | data formatting | bytes 131072 | tf_op jit(solution)/shard_map/pallas_call | solution.py:338
  42.8 0.6 %copy.11 = f32[64,256]{1,0:T(8,128)} copy(f32[64,256]{1,0:T(8,128)S(1)} %get-tuple-element.9) | data formatting | bytes 131072
  43.4 0.6 %copy.12 = bf16[64,256]{1,0:T(8,128)(2,1)} copy(bf16[64,256]{1,0:T(8,128)(2,1)S(1)} %get-tuple-element.11) | data formatting | bytes 65536
Async XLA Ops:
  0.6 1.0 %copy-start.1 = (bf16[384,256]{1,0:T(8,128)(2,1)S(1)}, bf16[384,256]{1,0:T(8,128)(2,1)}, u32[]{:S(2)}) copy-start(bf16[384,256]{1,0:T(8,128)(2,1)} %x_ref.1) | copy-start | bytes 589828
  1.6 1.0 %copy-start = (bf16[384,512]{1,0:T(8,128)(2,1)S(1)}, bf16[384,512]{1,0:T(8,128)(2,1)}, u32[]{:S(2)}) copy-start(bf16[384,512]{1,0:T(8,128)(2,1)} %c_ref.1) | copy-start | bytes 1179652
  2.6 0.8 %copy-start.2 = (f32[64,256]{1,0:T(8,128)S(1)}, f32[64,256]{1,0:T(8,128)}, u32[]{:S(2)}) copy-start(f32[64,256]{1,0:T(8,128)} %m_ref.1) | copy-start | bytes 196612

commit v2 on v1

--- a/solution.py
+++ b/solution.py
@@ -10,6 +10,7 @@
 MESH = pl.DeviceIdType.MESH
 F32, BF16 = jnp.float32, jnp.bfloat16
 SUB, LANE = 8, 128
+SLICES, CUTS = 8, (2, 6)
 NT = (((1,), (1,)), ((), ()))
 NN = (((1,), (0,)), ((), ()))
 TN = (((0,), (0,)), ((), ()))
@@ -17,14 +18,19 @@
 
 def split(x):
     hi = x.astype(BF16)
-    lo = (x - hi.astype(F32)).astype(BF16)
-    return jnp.concatenate([hi, lo], axis=0)
+    rest = x - hi.astype(F32)
+    mid = rest.astype(BF16)
+    low = (rest - mid.astype(F32)).astype(BF16)
+    return jnp.concatenate([hi, mid, low], axis=0)
+
+
+def fold(both):
+    rows = both.shape[0] // 3
+    return both[:rows] + (both[rows : 2 * rows] + both[2 * rows :])
 
 
 def dot_split(x, y, dims):
-    rows = x.shape[0]
-    both = lax.dot_general(split(x), y, dims, preferred_element_type=F32)
-    return both[:rows] + both[rows:]
+    return fold(lax.dot_general(split(x), y, dims, preferred_element_type=F32))
 
 
 def dot_high(x, y, dims):
@@ -68,20 +74,21 @@
 
 def kernel(
     n_rep, n_shard, scale_factor,
-    x_ref, c_ref, m_ref, q_ref,
-    mom_out, right_out, up_out,
-    left_part, left_in, left, ortho, right_part, right_in, right, sq_in, grad_part, grad_in, pad, turn,
-    send, recv,
+    x_hbm, c_hbm, m_hbm, q_hbm,
+    out_ref,
+    left_part, left_in, left, right_part, right_in, right, sq_in, grad_part, grad_in, pad, turn,
+    x_ref, c_ref, m_ref, q_ref, send, recv, load,
 ):
     rep, shard = lax.axis_index("rep"), lax.axis_index("shard")
     n_dev = n_rep * n_shard
     me = rep * n_shard + shard
-    rank = q_ref.shape[1]
+    rank = q_ref.shape[0]
     out_total = c_ref.shape[1]
     rows, feats = m_ref.shape
     row_blocks = rank // SUB
     left_owners = row_blocks * (out_total // LANE)
-    right_owners = row_blocks
+    share = max(SUB, LANE // n_rep)
+    right_owners = LANE // share
     chunk = min(512, out_total)
     n_chunk = out_total // chunk
     per_tile = LANE // rows
@@ -121,7 +128,14 @@
         return ref.at[pl.ds(r, SUB), pl.ds(c, LANE)]
 
     def band(b):
-        return pl.ds(pl.multiple_of(b * SUB, SUB), SUB)
+        return pl.ds(pl.multiple_of(b * share, SUB), share)
+
+    loads = [
+        pltpu.make_async_copy(src, dst, load.at[i])
+        for i, (src, dst) in enumerate(((q_hbm, q_ref), (x_hbm, x_ref), (m_hbm, m_ref), (c_hbm, c_ref)))
+    ]
+    for each in loads:
+        each.start()
 
     barrier = pltpu.get_barrier_semaphore()
 
@@ -131,14 +145,18 @@
 
     lax.fori_loop(1, n_dev, greet, 0)
 
+    loads[0].wait()
+    loads[1].wait()
     x = x_ref[...]
-    q_t = q_ref[...].T
+    q_t = q_ref[...]
     w_t = dot_split(q_t, x, NT)
-    w_two = split(w_t)
+    w_terms = split(w_t)
+    loads[2].wait()
+    loads[3].wait()
 
     def left_chunk(i):
-        both = lax.dot_general(w_two, c_ref[:, lanes(i)], NN, preferred_element_type=F32)
-        left_part[:, lanes(i)] = both[:rank] + both[rank:]
+        both = lax.dot_general(w_terms, c_ref[:, lanes(i)], NN, preferred_element_type=F32)
+        left_part[:, lanes(i)] = fold(both)
 
     over(n_chunk, left_chunk)
     pad[...] = jnp.zeros_like(pad)
@@ -157,11 +175,30 @@
 
     lax.fori_loop(1, n_dev, send_left, 0)
 
+    step = rows // SLICES
+
+    def grad_rows(r):
+        return pl.ds(pl.multiple_of(r * rows, rows), rows)
+
+    def send_grad(first, last):
+        if first == last:
+            return
+
+        def one(p, u):
+            t = lax.rem(rep + p, n_rep)
+            n = (last - first) * step
+            src = pl.ds(pl.multiple_of(t * rows + first * step, SUB), n)
+            copy(grad_part.at[src, :], grad_in.at[rep, pl.ds(first * step, n), :], 2, (t, shard)).start()
+            return u
+
+        lax.fori_loop(1, n_rep, one, 0)
+
     def grad_chunk(i):
         g = lax.dot_general(c_ref[:, lanes(i)], x, TN, preferred_element_type=F32)
         grad_part[lanes(i), :] = g
 
     over(n_chunk, grad_chunk)
+    send_grad(0, CUTS[0])
 
     def own_left():
         left_in[me] = tile(left_part, me)[...]
@@ -176,20 +213,10 @@
 
     guarded(left_owners, n_dev, me, own_left)
 
-    def grad_rows(r):
-        return pl.ds(pl.multiple_of(r * rows, rows), rows)
-
-    def send_grad(p, u):
-        t = lax.rem(rep + p, n_rep)
-        copy(grad_part.at[grad_rows(t), :], grad_in.at[rep], 2, (t, shard)).start()
-        return u
-
+    send_grad(CUTS[0], CUTS[1])
     if left_owners == n_dev:
         drain(recv.at[1], left_in.at[pl.ds(0, n_dev - 1)])
-        lax.fori_loop(1, n_rep, send_grad, 0)
-    else:
-        lax.fori_loop(1, n_rep, send_grad, 0)
-
+    else:
         @pl.when(me < left_owners)
         def _():
             drain(recv.at[1], left_in.at[pl.ds(0, left_owners - 1)])
@@ -201,32 +228,16 @@
     grad_in[rep] = grad_part[grad_rows(rep), :]
 
     if n_chunk == 1:
-        whole = left[...]
-        gram = dot_high(whole, whole, NT)
-    else:
-        gram = lax.fori_loop(
-            0, n_chunk,
-            lambda i, g: g + dot_high(left[:, lanes(i)], left[:, lanes(i)], NT),
-            jnp.zeros((rank, rank), F32),
-        )
-    inv = inverse_factor(gram)
-
-    def ortho_chunk(i):
-        ortho[:, lanes(i)] = dot_high(inv, left[:, lanes(i)], NN)
-
-    over(n_chunk, ortho_chunk)
-    if n_chunk == 1:
-        v_t = dot_split(ortho[...], c_ref[...], NT)
+        v_t = dot_split(left[...], c_ref[...], NT)
     else:
         v_t = lax.fori_loop(
             0, n_chunk,
-            lambda i, v: v + dot_split(ortho[:, lanes(i)], c_ref[:, lanes(i)], NT),
+            lambda i, v: v + dot_split(left[:, lanes(i)], c_ref[:, lanes(i)], NT),
             jnp.zeros((rank, c_ref.shape[0]), F32),
         )
-    mine_t = ortho[:, my_lanes]
-    right_part[...] = dot_split(v_t, x, NN) + dot_high(
-        mine_t, pad[...], NN
-    )
+    mine_t = left[:, my_lanes]
+    cross_t = dot_split(v_t, x, NN) + dot_high(mine_t, pad[...], NN)
+    right_part[...] = jnp.concatenate([cross_t[:, :LANE], cross_t[:, LANE:]], axis=0).T
 
     def send_right(p, u):
         t = lax.rem(rep + p, n_rep)
@@ -237,14 +248,31 @@
         return u
 
     lax.fori_loop(1, n_rep, send_right, 0)
-    pad_turn = mine_t.T
+    send_grad(CUTS[1], SLICES)
+
+    if n_chunk == 1:
+        whole = left[...]
+        gram = dot_high(whole, whole, NT)
+    else:
+        gram = lax.fori_loop(
+            0, n_chunk,
+            lambda i, g: g + dot_high(left[:, lanes(i)], left[:, lanes(i)], NT),
+            jnp.zeros((rank, rank), F32),
+        )
+    inv = inverse_factor(gram)
+    turn[...] = mine_t.T
+    mine = dot_high(turn[my_rows, :], inv, NT)
+    none = jnp.zeros((rank, rank), F32)
+    inv_two = jnp.concatenate(
+        [jnp.concatenate([inv, none], axis=1), jnp.concatenate([none, inv], axis=1)], axis=0
+    )
 
     def own_right():
         right_in[rep] = right_part[band(rep), :]
         drain(recv.at[3], right_in.at[pl.ds(0, n_rep - 1)])
-        total = jnp.sum(right_in[...], axis=0)
+        total = dot_high(jnp.sum(right_in[...], axis=0), inv_two, NT)
         right[band(rep), :] = total
-        sq_in[shard, band(rep), :] = jnp.broadcast_to(jnp.sum(total * total, axis=1, keepdims=True), (SUB, LANE))
+        sq_in[me] = jnp.broadcast_to(jnp.sum(total * total, axis=0, keepdims=True), (SUB, LANE))
 
         def give_right(p, u):
             copy(right.at[band(rep), :], right.at[band(rep), :], 4, (lax.rem(rep + p, n_rep), shard)).start()
@@ -253,8 +281,7 @@
         lax.fori_loop(1, n_rep, give_right, 0)
 
         def give_sq(p, u):
-            place = sq_in.at[shard, band(rep), :]
-            copy(place, place, 5, device(lax.rem(me + p, n_dev))).start()
+            copy(sq_in.at[me], sq_in.at[me], 5, device(lax.rem(me + p, n_dev))).start()
             return u
 
         lax.fori_loop(1, n_dev, give_sq, 0)
@@ -263,8 +290,6 @@
 
     drain(recv.at[2], grad_in.at[pl.ds(0, n_rep - 1)])
     blended = m_ref[...] + lax.fori_loop(1, n_rep, lambda r, g: g + grad_in[r], grad_in[0])
-    turn[...] = pad_turn
-    mine = turn[my_rows, :]
 
     def finish_recv(n_right, n_sq):
         drain(recv.at[4], right_in.at[pl.ds(0, n_right)])
@@ -283,14 +308,19 @@
         def _():
             finish_recv(right_owners, sq_all)
 
-    right_t = right[...]
-    mom_out[...] = blended - 0.05 * dot_high(mine, right_t, NN)
-    norm = jnp.sqrt(jnp.sum(sq_in[...], axis=0) + 1e-06)
-    factor_t = jnp.concatenate(
-        [right_t[:, LANE * i : LANE * (i + 1)] / norm for i in range(feats // LANE)], axis=1
-    )
-    up_out[...] = (scale_factor * dot_high(mine, factor_t, NN)).astype(up_out.dtype)
-    right_out[...] = factor_t.T
+    def wide(packed):
+        t = packed.T
+        return jnp.concatenate([t[:rank], t[rank:]], axis=1)
+
+    packed = right[...]
+    right_t = wide(packed)
+    out_ref[0] = blended - 0.05 * dot_high(mine, right_t, NN)
+    halves = jnp.sum(jnp.sum(sq_in[pl.ds(0, sq_all)], axis=0), axis=0, keepdims=True) * (1.0 / SUB)
+    column_sq = halves[:, :rank] + halves[:, rank:]
+    norm = jnp.sqrt(column_sq + 1e-06)
+    factor_t = wide(packed / jnp.concatenate([norm, norm], axis=1))
+    out_ref[2] = scale_factor * dot_high(mine, factor_t, NN)
+    out_ref[1] = factor_t
 
     def left_sent(n):
         drain(send.at[0], left_in.at[pl.ds(0, n)])
@@ -334,36 +364,39 @@
     rank = right_prev.shape[1]
     n_dev = n_rep * n_shard
     scale_factor = (out_total * feats * n_shard / rank) ** 0.5
+    share = max(SUB, LANE // n_rep)
+    assert 2 * rank == LANE and feats == 2 * LANE
     vmem = pl.BlockSpec(memory_space=pltpu.VMEM)
-    return pl.pallas_call(
+    results = pl.pallas_call(
         functools.partial(kernel, n_rep, n_shard, scale_factor),
-        out_shape=(
-            jax.ShapeDtypeStruct((rows, feats), F32),
-            jax.ShapeDtypeStruct((feats, rank), F32),
-            jax.ShapeDtypeStruct((rows, feats), BF16),
-        ),
-        in_specs=[vmem] * 4,
-        out_specs=(vmem,) * 3,
+        out_shape=jax.ShapeDtypeStruct((3, rows, feats), F32),
+        in_specs=[pl.BlockSpec(memory_space=pltpu.HBM)] * 4,
+        out_specs=vmem,
         scratch_shapes=[
             pltpu.VMEM((rank, out_total), F32),
             pltpu.VMEM((n_dev, SUB, LANE), F32),
             pltpu.VMEM((rank, out_total), F32),
-            pltpu.VMEM((rank, out_total), F32),
-            pltpu.VMEM((rank, feats), F32),
-            pltpu.VMEM((n_rep, SUB, feats), F32),
-            pltpu.VMEM((rank, feats), F32),
-            pltpu.VMEM((n_shard, rank, LANE), F32),
+            pltpu.VMEM((LANE, LANE), F32),
+            pltpu.VMEM((n_rep, share, LANE), F32),
+            pltpu.VMEM((LANE, LANE), F32),
+            pltpu.VMEM((n_dev, SUB, LANE), F32),
             pltpu.VMEM((out_total, feats), F32),
             pltpu.VMEM((n_rep, rows, feats), F32),
             pltpu.VMEM((LANE, feats), F32),
             pltpu.VMEM((LANE, rank), F32),
+            pltpu.VMEM(inputs.shape, BF16),
+            pltpu.VMEM(cotangent.shape, BF16),
+            pltpu.VMEM(momentum.shape, F32),
+            pltpu.VMEM((rank, feats), F32),
             pltpu.SemaphoreType.DMA((6,)),
             pltpu.SemaphoreType.DMA((6,)),
+            pltpu.SemaphoreType.DMA((4,)),
         ],
         compiler_params=pltpu.CompilerParams(
-            collective_id=0, has_side_effects=True, vmem_limit_bytes=48 * 1024 * 1024
+            collective_id=0, has_side_effects=True, vmem_limit_bytes=67043328
         ),
-    )(inputs, cotangent, momentum, right_prev)
+    )(inputs, cotangent, momentum, right_prev.T)
+    return results[0], results[1].T, results[2].astype(BF16)
 
 
 def solution(mesh):

time: 44.2 us -> 38.6 us (0.87)
  Pallas kernels: 38.6 us -> 34.7 us
  local copies, waits for them, and re-layouts: 4.76 us -> 2.99 us
    unnamed x9 -> x0, local copies, waits for them, and re-layouts: 4.05 us -> none
    pallas_call x1, Pallas kernels: 38.6 us -> 34.7 us  [body(): pl.pallas_call(functools.partial(kernel, n_rep, n_shard, scale_factor), o...]
    transpose x0 -> x1, local copies, waits for them, and re-layouts: none -> 1.53 us  [body(): return (results[0], results[1].T, results[2].astype(BF16))]
    convert_element_type x0 -> x1, local copies, waits for them, and re-layouts: none -> 1.46 us  [body(): return (results[0], results[1].T, results[2].astype(BF16))]
    pallas_call x1 -> x0, local copies, waits for them, and re-layouts: 0.71 us -> none  [body(): pl.pallas_call(functools.partial(kernel, n_rep, n_shard, scale_factor), o...]
where the time goes in v2:
time: 38.6 us; the launch traced here: 38.4 us
  Pallas kernels  34.7 us (90%)
  local copies, waits for them, and re-layouts  2.99 us (8%)
  between operations  0.64 us (2%)
    pallas_call x1, Pallas kernels, body(): pl.pallas_call(functools.partial(kernel, n_rep, n_shard, scale_factor), o...  34.7 us
    transpose x1, local copies, waits for them, and re-layouts, body(): return (results[0], results[1].T, results[2].astype(BF16))  1.53 us
    convert_element_type x1, local copies, waits for them, and re-layouts, body(): return (results[0], results[1].T, results[2].astype(BF16))  1.46 us

profile of v2, /device:TPU:0, one launch (start us, length us, event | category | flops | bytes accessed | tf_op | source)
XLA Modules:
  0.0 38.4 jit_solution(10932295495298572380)
XLA Ops:
  0.6 34.7 %shard_map.67 = f32[3,64,256]{2,1,0:T(8,128)} custom-call(bf16[384,256]{1,0:T(8,128)(2,1)} %x_hbm.1, bf16[384,512]{1,0:T(8,128)(2,1)} %c_hbm.1, f32[64,256]{1,0:T(8,128)} %m_hbm.1, f32[64,256]{1,0:T(8,128)} %bitcast.9), custom_call_target="tpu_custom_call" | custom-call | tf_op jit(solution)/shard_map/pallas_call | solution.py:370
  35.4 1.5 %slice_bitcast_fusion = (f32[256,64]{0,1:T(8,128)}, f32[64,256]{1,0:T(8,128)}) fusion(f32[3,64,256]{2,1,0:T(8,128)} %shard_map.67), kind=kLoop, calls=%fused_computation.1 | loop fusion | bytes 262144 | tf_op jit(solution)/shard_map/transpose | solution.py:399
  36.9 1.5 %fusion = bf16[64,256]{1,0:T(8,128)(2,1)} fusion(f32[3,64,256]{2,1,0:T(8,128)} %shard_map.67), kind=kLoop, calls=%fused_computation.3 | loop fusion | bytes 65536 | tf_op jit(solution)/shard_map/convert_element_type | solution.py:399

commit v3 on v2

--- a/solution.py
+++ b/solution.py
@@ -10,7 +10,7 @@
 MESH = pl.DeviceIdType.MESH
 F32, BF16 = jnp.float32, jnp.bfloat16
 SUB, LANE = 8, 128
-SLICES, CUTS = 8, (2, 6)
+UNIT, PAIR_CUT, LINE_CUTS = 8, 4, (0, 8)
 NT = (((1,), (1,)), ((), ()))
 NN = (((1,), (0,)), ((), ()))
 TN = (((0,), (0,)), ((), ()))
@@ -76,7 +76,7 @@
     n_rep, n_shard, scale_factor,
     x_hbm, c_hbm, m_hbm, q_hbm,
     out_ref,
-    left_part, left_in, left, right_part, right_in, right, sq_in, grad_part, grad_in, pad, turn,
+    left_part, left_in, left, right_part, right_in, right, sq_in, grad_part, grad_in, pair_in, pair_sum, pad, turn,
     x_ref, c_ref, m_ref, q_ref, send, recv, load,
 ):
     rep, shard = lax.axis_index("rep"), lax.axis_index("shard")
@@ -175,30 +175,55 @@
 
     lax.fori_loop(1, n_dev, send_left, 0)
 
-    step = rows // SLICES
-
-    def grad_rows(r):
-        return pl.ds(pl.multiple_of(r * rows, rows), rows)
-
-    def send_grad(first, last):
+    n_line = n_rep // 2
+    line, side = rep // 2, lax.rem(rep, 2)
+    unit = rows // UNIT
+
+    def span(first, last):
+        return pl.ds(first * unit, (last - first) * unit)
+
+    def send_pair(first, last, k):
         if first == last:
             return
+        part = span(first, last)
+        copy(
+            grad_part.at[1 - side, :, part, :], pair_in.at[:, part, :], k, (2 * line + 1 - side, shard)
+        ).start()
+
+    def take_pair(first, last, k):
+        if first == last:
+            return
+        part = span(first, last)
+        drain(recv.at[k], pair_in.at[:, part, :])
+        for h in range(n_line) if n_line <= 8 else ():
+            pair_sum[h, part, :] = grad_part[side, h, part, :] + pair_in[h, part, :]
+        if n_line > 8:
+            def add(h, u):
+                pair_sum[h, part, :] = grad_part[side, h, part, :] + pair_in[h, part, :]
+                return u
+
+            lax.fori_loop(0, n_line, add, 0)
+
+    def send_line(first, last):
+        if first == last:
+            return
+        part = span(first, last)
 
         def one(p, u):
-            t = lax.rem(rep + p, n_rep)
-            n = (last - first) * step
-            src = pl.ds(pl.multiple_of(t * rows + first * step, SUB), n)
-            copy(grad_part.at[src, :], grad_in.at[rep, pl.ds(first * step, n), :], 2, (t, shard)).start()
+            t = lax.rem(line + p, n_line)
+            copy(pair_sum.at[t, part, :], grad_in.at[line, part, :], 2, (2 * t + side, shard)).start()
             return u
 
-        lax.fori_loop(1, n_rep, one, 0)
+        lax.fori_loop(1, n_line, one, 0)
 
     def grad_chunk(i):
         g = lax.dot_general(c_ref[:, lanes(i)], x, TN, preferred_element_type=F32)
-        grad_part[lanes(i), :] = g
+        for r in range(chunk // rows):
+            at = i * (chunk // rows) + r
+            grad_part[at % 2, at // 2] = g[r * rows : (r + 1) * rows]
 
     over(n_chunk, grad_chunk)
-    send_grad(0, CUTS[0])
+    send_pair(0, PAIR_CUT, 6)
 
     def own_left():
         left_in[me] = tile(left_part, me)[...]
@@ -213,7 +238,7 @@
 
     guarded(left_owners, n_dev, me, own_left)
 
-    send_grad(CUTS[0], CUTS[1])
+    send_pair(PAIR_CUT, UNIT, 7)
     if left_owners == n_dev:
         drain(recv.at[1], left_in.at[pl.ds(0, n_dev - 1)])
     else:
@@ -225,7 +250,9 @@
         def _():
             drain(recv.at[1], left_in.at[pl.ds(0, left_owners)])
 
-    grad_in[rep] = grad_part[grad_rows(rep), :]
+
+    take_pair(0, PAIR_CUT, 6)
+    send_line(0, LINE_CUTS[0])
 
     if n_chunk == 1:
         v_t = dot_split(left[...], c_ref[...], NT)
@@ -248,7 +275,8 @@
         return u
 
     lax.fori_loop(1, n_rep, send_right, 0)
-    send_grad(CUTS[1], SLICES)
+    take_pair(PAIR_CUT, UNIT, 7)
+    send_line(LINE_CUTS[0], LINE_CUTS[1])
 
     if n_chunk == 1:
         whole = left[...]
@@ -272,7 +300,7 @@
         drain(recv.at[3], right_in.at[pl.ds(0, n_rep - 1)])
         total = dot_high(jnp.sum(right_in[...], axis=0), inv_two, NT)
         right[band(rep), :] = total
-        sq_in[me] = jnp.broadcast_to(jnp.sum(total * total, axis=0, keepdims=True), (SUB, LANE))
+        sq_in[me] = jnp.sum(total * total, axis=0, keepdims=True)
 
         def give_right(p, u):
             copy(right.at[band(rep), :], right.at[band(rep), :], 4, (lax.rem(rep + p, n_rep), shard)).start()
@@ -288,12 +316,15 @@
 
     guarded(right_owners, n_rep, rep, own_right)
 
-    drain(recv.at[2], grad_in.at[pl.ds(0, n_rep - 1)])
-    blended = m_ref[...] + lax.fori_loop(1, n_rep, lambda r, g: g + grad_in[r], grad_in[0])
+    send_line(LINE_CUTS[1], UNIT)
+
+    grad_in[line] = pair_sum[line]
+    drain(recv.at[2], grad_in.at[pl.ds(0, n_line - 1)])
+    blended = m_ref[...] + lax.fori_loop(1, n_line, lambda r, g: g + grad_in[r], grad_in[0])
 
     def finish_recv(n_right, n_sq):
         drain(recv.at[4], right_in.at[pl.ds(0, n_right)])
-        flat = left_in.at[pl.ds(0, n_sq)]
+        flat = sq_in.at[pl.ds(0, n_sq)]
         drain(recv.at[5], flat)
 
     sq_all = right_owners * n_shard
@@ -315,7 +346,7 @@
     packed = right[...]
     right_t = wide(packed)
     out_ref[0] = blended - 0.05 * dot_high(mine, right_t, NN)
-    halves = jnp.sum(jnp.sum(sq_in[pl.ds(0, sq_all)], axis=0), axis=0, keepdims=True) * (1.0 / SUB)
+    halves = jnp.sum(sq_in[pl.ds(0, sq_all)], axis=0)
     column_sq = halves[:, :rank] + halves[:, rank:]
     norm = jnp.sqrt(column_sq + 1e-06)
     factor_t = wide(packed / jnp.concatenate([norm, norm], axis=1))
@@ -338,11 +369,14 @@
         def _():
             left_sent(left_owners)
 
-    drain(send.at[2], grad_in.at[pl.ds(0, n_rep - 1)])
+    drain(send.at[2], grad_in.at[pl.ds(0, n_line - 1)])
+    for first, last, k in ((0, PAIR_CUT, 6), (PAIR_CUT, UNIT, 7)):
+        if first < last:
+            drain(send.at[k], pair_in.at[:, span(first, last), :])
 
     def right_sent():
         drain(send.at[4], right_in.at[pl.ds(0, n_rep - 1)])
-        drain(send.at[5], left_in.at[pl.ds(0, n_dev - 1)])
+        drain(send.at[5], sq_in.at[pl.ds(0, n_dev - 1)])
 
     if right_owners == n_rep:
         drain(send.at[3], right_in.at[pl.ds(0, n_rep - 1)])
@@ -365,11 +399,11 @@
     n_dev = n_rep * n_shard
     scale_factor = (out_total * feats * n_shard / rank) ** 0.5
     share = max(SUB, LANE // n_rep)
-    assert 2 * rank == LANE and feats == 2 * LANE
+    assert 2 * rank == LANE and feats == 2 * LANE and n_rep % 2 == 0
     vmem = pl.BlockSpec(memory_space=pltpu.VMEM)
     results = pl.pallas_call(
         functools.partial(kernel, n_rep, n_shard, scale_factor),
-        out_shape=jax.ShapeDtypeStruct((3, rows, feats), F32),
+        out_shape=pltpu.VMEM((3, rows, feats), F32),
         in_specs=[pl.BlockSpec(memory_space=pltpu.HBM)] * 4,
         out_specs=vmem,
         scratch_shapes=[
@@ -379,21 +413,23 @@
             pltpu.VMEM((LANE, LANE), F32),
             pltpu.VMEM((n_rep, share, LANE), F32),
             pltpu.VMEM((LANE, LANE), F32),
-            pltpu.VMEM((n_dev, SUB, LANE), F32),
-            pltpu.VMEM((out_total, feats), F32),
-            pltpu.VMEM((n_rep, rows, feats), F32),
+            pltpu.VMEM((n_dev, 1, LANE), F32),
+            pltpu.VMEM((2, n_rep // 2, rows, feats), F32),
+            pltpu.VMEM((n_rep // 2, rows, feats), F32),
+            pltpu.VMEM((n_rep // 2, rows, feats), F32),
+            pltpu.VMEM((n_rep // 2, rows, feats), F32),
             pltpu.VMEM((LANE, feats), F32),
             pltpu.VMEM((LANE, rank), F32),
             pltpu.VMEM(inputs.shape, BF16),
             pltpu.VMEM(cotangent.shape, BF16),
             pltpu.VMEM(momentum.shape, F32),
             pltpu.VMEM((rank, feats), F32),
-            pltpu.SemaphoreType.DMA((6,)),
-            pltpu.SemaphoreType.DMA((6,)),
+            pltpu.SemaphoreType.DMA((8,)),
+            pltpu.SemaphoreType.DMA((8,)),
             pltpu.SemaphoreType.DMA((4,)),
         ],
         compiler_params=pltpu.CompilerParams(
-            collective_id=0, has_side_effects=True, vmem_limit_bytes=67043328
+            collective_id=0, has_side_effects=True, vmem_limit_bytes=60000000
         ),
     )(inputs, cotangent, momentum, right_prev.T)
     return results[0], results[1].T, results[2].astype(BF16)

time: 38.6 us -> 32.5 us (0.84)
  Pallas kernels: 34.7 us -> 30.4 us
  local copies, waits for them, and re-layouts: 2.99 us -> 1.28 us
    pallas_call x1, Pallas kernels: 34.7 us -> 30.4 us  [body(): pl.pallas_call(functools.partial(kernel, n_rep, n_shard, scale_factor), o...]
    transpose x1, local copies, waits for them, and re-layouts: 1.53 us -> 0.66 us  [body(): return (results[0], results[1].T, results[2].astype(BF16))]
    convert_element_type x1, local copies, waits for them, and re-layouts: 1.46 us -> 0.62 us  [body(): return (results[0], results[1].T, results[2].astype(BF16))]
where the time goes in v3:
time: 32.5 us; the launch traced here: 32.3 us
  Pallas kernels  30.4 us (94%)
  local copies, waits for them, and re-layouts  1.28 us (4%)
  between operations  0.64 us (2%)
    pallas_call x1, Pallas kernels, body(): pl.pallas_call(functools.partial(kernel, n_rep, n_shard, scale_factor), o...  30.4 us
    transpose x1, local copies, waits for them, and re-layouts, body(): return (results[0], results[1].T, results[2].astype(BF16))  0.66 us

profile of v3, /device:TPU:0, one launch (start us, length us, event | category | flops | bytes accessed | tf_op | source)
XLA Modules:
  0.0 32.3 jit_solution(16413246693039019055)
XLA Ops:
  0.6 30.4 %shard_map.67 = f32[3,64,256]{2,1,0:T(8,128)S(1)} custom-call(bf16[384,256]{1,0:T(8,128)(2,1)} %x_hbm.1, bf16[384,512]{1,0:T(8,128)(2,1)} %c_hbm.1, f32[64,256]{1,0:T(8,128)} %m_hbm.1, f32[64,256]{1,0:T(8,128)} %bitcast.9), custom_call_target="tpu_custom_call" | custom-call | tf_op jit(solution)/shard_map/pallas_call | solution.py:404
  31.0 0.7 %slice_bitcast_fusion = (f32[256,64]{0,1:T(8,128)}, f32[64,256]{1,0:T(8,128)}) fusion(f32[3,64,256]{2,1,0:T(8,128)S(1)} %shard_map.67), kind=kLoop, calls=%fused_computation.1 | loop fusion | bytes 262144 | tf_op jit(solution)/shard_map/transpose | solution.py:435
  31.7 0.6 %fusion = bf16[64,256]{1,0:T(8,128)(2,1)} fusion(f32[3,64,256]{2,1,0:T(8,128)S(1)} %shard_map.67), kind=kLoop, calls=%fused_computation.3 | loop fusion | bytes 65536 | tf_op jit(solution)/shard_map/convert_element_type | solution.py:435

commit v4 on v3

--- a/solution.py
+++ b/solution.py
@@ -10,7 +10,7 @@
 MESH = pl.DeviceIdType.MESH
 F32, BF16 = jnp.float32, jnp.bfloat16
 SUB, LANE = 8, 128
-UNIT, PAIR_CUT, LINE_CUTS = 8, 4, (0, 8)
+UNIT, PAIR_CUT, LINE_CUTS = 8, 4, (0, 6)
 NT = (((1,), (1,)), ((), ()))
 NN = (((1,), (0,)), ((), ()))
 TN = (((0,), (0,)), ((), ()))
@@ -251,9 +251,6 @@
             drain(recv.at[1], left_in.at[pl.ds(0, left_owners)])
 
 
-    take_pair(0, PAIR_CUT, 6)
-    send_line(0, LINE_CUTS[0])
-
     if n_chunk == 1:
         v_t = dot_split(left[...], c_ref[...], NT)
     else:
@@ -275,6 +272,7 @@
         return u
 
     lax.fori_loop(1, n_rep, send_right, 0)
+    take_pair(0, PAIR_CUT, 6)
     take_pair(PAIR_CUT, UNIT, 7)
     send_line(LINE_CUTS[0], LINE_CUTS[1])
 

time: 32.5 us -> 32.1 us (0.988)
  Pallas kernels: 30.4 us -> 30 us
    pallas_call x1, Pallas kernels: 30.4 us -> 30 us  [body(): pl.pallas_call(functools.partial(kernel, n_rep, n_shard, scale_factor), o...]
where the time goes in v4:
time: 32.1 us; the launch traced here: 32 us
  Pallas kernels  30 us (93%)
  local copies, waits for them, and re-layouts  1.28 us (4%)
  between operations  0.64 us (2%)
    pallas_call x1, Pallas kernels, body(): pl.pallas_call(functools.partial(kernel, n_rep, n_shard, scale_factor), o...  30 us
    transpose x1, local copies, waits for them, and re-layouts, body(): return (results[0], results[1].T, results[2].astype(BF16))  0.66 us

profile of v4, /device:TPU:0, one launch (start us, length us, event | category | flops | bytes accessed | tf_op | source)
XLA Modules:
  0.0 32.0 jit_solution(9431335507727372144)
XLA Ops:
  0.6 30.0 %shard_map.67 = f32[3,64,256]{2,1,0:T(8,128)S(1)} custom-call(bf16[384,256]{1,0:T(8,128)(2,1)} %x_hbm.1, bf16[384,512]{1,0:T(8,128)(2,1)} %c_hbm.1, f32[64,256]{1,0:T(8,128)} %m_hbm.1, f32[64,256]{1,0:T(8,128)} %bitcast.9), custom_call_target="tpu_custom_call" | custom-call | tf_op jit(solution)/shard_map/pallas_call | solution.py:402
  30.7 0.7 %slice_bitcast_fusion = (f32[256,64]{0,1:T(8,128)}, f32[64,256]{1,0:T(8,128)}) fusion(f32[3,64,256]{2,1,0:T(8,128)S(1)} %shard_map.67), kind=kLoop, calls=%fused_computation.1 | loop fusion | bytes 262144 | tf_op jit(solution)/shard_map/transpose | solution.py:433
  31.3 0.6 %fusion = bf16[64,256]{1,0:T(8,128)(2,1)} fusion(f32[3,64,256]{2,1,0:T(8,128)S(1)} %shard_map.67), kind=kLoop, calls=%fused_computation.3 | loop fusion | bytes 65536 | tf_op jit(solution)/shard_map/convert_element_type | solution.py:433
